TPU v7x, 32 devices: a whole 2x2x4 slice. The times are simulated.
32 devices in a mesh: tok: 4 (over y, x), col: 8 (over z, core).
Axes of the slice: x: 2, y: 2, z: 4, core: 2. Of those that a mesh axis runs over, the one named last changes fastest.
Arguments:
- activations: bfloat16 [8192, 8192], P('tok', 'col'), may hold values from -60 to 60, as said below
- weight: bfloat16 [8192, 8192], P('tok', 'col'), may hold values from -6 to 6
- keep_mask: int32 [8192, 8192], P('tok', 'col'), may hold values from 0 to 1
Outputs:
- new_weight: bfloat16 [8192, 8192], P('tok', 'col')
Inputs may be any that keep to these rules, and one draw needn't show every extreme that they name: activations of calibration tokens.
All inputs are finite; a program needn't handle non-finite values.
Results may differ from a plain program's by a relative error of at most 0.00115.
Values may be sent and summed in bfloat16 or wider, within the bound.
No kernel may reach another device: no remote copies, remote signals or barrier semaphores. Data moves between devices by JAX's collectives and lax.ppermute only.
A program may use at most 128 MiB of HBM per device.

v0:
```python
import jax
import jax.numpy as jnp
from jax import lax
from jax.sharding import PartitionSpec as P

B = 1024
ITERS = 4


def per_device(activations, weight, keep_mask):
    highest = lax.Precision.HIGHEST
    n_col = lax.axis_size("col")
    n_tok = lax.axis_size("tok")
    tok_rows = activations.shape[0]
    panel_width = B // n_col
    total_count = tok_rows * n_tok
    partial_panel = lax.dot_general(
        activations,
        lax.all_gather(activations[:, :panel_width], "col", axis=1, tiled=True),
        (((0,), (0,)), ((), ())),
        preferred_element_type=jnp.float32,
    )
    block_part = lax.psum(partial_panel[:panel_width], "tok") / total_count
    diagonal_block = lax.all_gather(block_part, "col", axis=0, tiled=True)
    identity = jnp.eye(B, dtype=jnp.float32)
    damping = 0.01 * jnp.mean(jnp.diagonal(diagonal_block))
    damped = diagonal_block + damping * identity
    frobenius = jnp.sqrt(jnp.sum(damped * damped))
    col_index = lax.axis_index("col")
    row_ids = col_index * panel_width + lax.iota(jnp.int32, panel_width)
    iterate = (row_ids[:, None] == lax.iota(jnp.int32, B)[None, :]).astype(jnp.float32) / frobenius
    for sweep in range(ITERS):
        if sweep == 0:
            whole = identity / frobenius
        else:
            whole = lax.all_gather(iterate.astype(jnp.bfloat16), "col", axis=0, tiled=True).astype(
                iterate.dtype
            )
        product = jnp.dot(iterate, damped, precision=highest)
        iterate = 2.0 * iterate - jnp.dot(product, whole, precision=highest)
    inverse = lax.all_gather(iterate, "col", axis=0, tiled=True)
    remainder = lax.psum(partial_panel[panel_width:], "tok") / total_count
    hessian_panel = jnp.concatenate([block_part, remainder], axis=0)
    pruned = jnp.where(
        keep_mask[:, :panel_width] == 0, weight[:, :panel_width], jnp.zeros((), jnp.bfloat16)
    )
    pruned_panel = lax.all_gather(pruned, "col", axis=1, tiled=True).astype(jnp.float32)
    factor_rows = jnp.dot(pruned_panel, inverse, precision=highest)
    correction = lax.dot_general(
        factor_rows, hessian_panel, (((1,), (1,)), ((), ())), precision=highest
    )
    kept = keep_mask.astype(jnp.float32)
    return (kept * (weight.astype(jnp.float32) - correction)).astype(jnp.bfloat16)


def solution(mesh):
    return jax.shard_map(
        per_device,
        mesh=mesh,
        in_specs=(P("tok", "col"), P("tok", "col"), P("tok", "col")),
        out_specs=P("tok", "col"),
        check_vma=False,
    )
```

profile of v0, /device:TPU:0, one launch (start us, length us, event | category | flops | bytes accessed | tf_op | source)
XLA Modules:
  0.0 493.3 jit_solution(1033233946870937970)
XLA Ops:
  6.5 0.0 all-gather.10.cloned.1.call-start
  6.5 1.9 slice.17
  8.4 0.0 all-gather.10.cloned.1.call-update
  8.4 0.0 all-reduce.3.cloned.1.call-start
  8.5 51.0 %all-gather.10.cloned.1.call-done = bf16[2048,1024]{1,0:T(8,128)(2,1)} async-done(((bf16[2048,128]{1,0:T(8,128)(2,1)}), bf16[2048,1024]{1,0:T(8,128)(2,1)}) %all-gather.10.cloned.1.call-update) | async-done | bytes 4194320 | tf_op jit(solution)/shard_map/all_gather | solution.py:19
  59.5 7.6 %fusion.31 = f32[1024,1024]{1,0:T(8,128)S(1)} fusion(bf16[2048,1024]{1,0:T(8,128)(2,1)} %param.3, bf16[2048,1024]{1,0:T(8,128)(2,1)} %all-gather.10.cloned.1.call-done), kind=kOutput, calls=%fused_computation.42 | convolution fusion | flops 4294967296 | bytes 12582912 | tf_op jit(solution)/shard_map/dot_general | solution.py:17
  67.1 0.8 slice.22
  67.9 2.3 slice.23
  70.2 0.0 all-reduce.3.cloned.1.call-update
  70.2 0.0 all-gather.12.cloned.1.call-start
  70.3 101.9 %all-reduce.3.cloned.1.call-done = (f32[128,1024]{1,0:T(8,128)}, f32[896,1024]{1,0:T(8,128)}) async-done(((f32[128,1024]{1,0:T(8,128)}, f32[896,1024]{1,0:T(8,128)}), (f32[128,1024]{1,0:T(8,128)}, f32[896,1024]{1,0:T(8,128)})) %all-reduce.3.cloned.1.call-update) | async-done | bytes 4194320 | tf_op jit(solution)/shard_map/psum | solution.py:23
  172.2 1.9 broadcast_multiply_fusion.1
  174.1 0.0 all-gather.12.cloned.1.call-update
  174.1 0.0 all-gather.14.cloned.1.call-start
  174.2 46.9 %all-gather.12.cloned.1.call-done = f32[1024,1024]{1,0:T(8,128)} async-done(((f32[128,1024]{1,0:T(8,128)}), f32[1024,1024]{1,0:T(8,128)}) %all-gather.12.cloned.1.call-update) | async-done | bytes 4194320 | tf_op jit(solution)/shard_map/all_gather | solution.py:24
  221.2 17.1 %gather_fusion = f32[1024]{0:T(1024)S(1)} fusion(f32[1024,1024]{1,0:T(8,128)} %all-gather.12.cloned.1.call-done, s32[1024]{0:T(1024)S(1)} %bitcast.16), kind=kCustom, calls=%fused_computation | custom fusion | bytes 16384 | tf_op jit(solution)/shard_map/jit(diagonal)/cond/branch_0_fun/gather | solution.py:26
  238.2 0.6 reduce_sum.18
  239.5 3.9 multiply_reduce_fusion
  244.0 4.7 fusion.16
  248.8 2.5 fusion.28
  251.3 0.0 all-gather.14.cloned.1.call-update
  251.3 0.0 all-gather.16.cloned.1.call-start
  251.3 4.7 fusion.15
  256.0 23.4 %all-gather.14.cloned.1.call-done = bf16[1024,1024]{1,0:T(8,128)(2,1)} async-done(((bf16[128,1024]{1,0:T(8,128)(2,1)}), bf16[1024,1024]{1,0:T(8,128)(2,1)}) %all-gather.14.cloned.1.call-update) | async-done | bytes 2097168 | tf_op jit(solution)/shard_map/all_gather | solution.py:36
  279.4 3.3 fusion.29
  282.7 0.0 all-gather.16.cloned.1.call-update
  282.8 0.2 all-gather.18.cloned.1.call-start
  283.0 4.7 fusion.14
  287.7 23.8 %all-gather.16.cloned.1.call-done = bf16[1024,1024]{1,0:T(8,128)(2,1)} async-done(((bf16[128,1024]{1,0:T(8,128)(2,1)}), bf16[1024,1024]{1,0:T(8,128)(2,1)}) %all-gather.16.cloned.1.call-update) | async-done | bytes 2097168 | tf_op jit(solution)/shard_map/all_gather | solution.py:36
  311.5 3.3 fusion.30
  314.9 0.0 all-gather.18.cloned.1.call-update
  314.9 0.0 all-gather.8.cloned.1.call-start
  314.9 2.3 fusion.17
  317.2 0.0 all-gather.8.cloned.1.call-update
  317.2 0.0 all-gather.20.cloned.1.call-start
  317.3 4.7 fusion.13
  322.0 21.6 %all-gather.18.cloned.1.call-done = bf16[1024,1024]{1,0:T(8,128)(2,1)} async-done(((bf16[128,1024]{1,0:T(8,128)(2,1)}), bf16[1024,1024]{1,0:T(8,128)(2,1)}) %all-gather.18.cloned.1.call-update) | async-done | bytes 2097168 | tf_op jit(solution)/shard_map/all_gather | solution.py:36
  343.6 3.4 convolution_subtract_fusion
  347.0 0.0 all-gather.20.cloned.1.call-update
  347.0 4.6 broadcast_multiply_fusion
  351.6 0.0 copy-start.1
  351.6 40.8 %all-gather.8.cloned.1.call-done = bf16[2048,1024]{1,0:T(8,128)(2,1)} async-done(((bf16[2048,128]{1,0:T(8,128)(2,1)}), bf16[2048,1024]{1,0:T(8,128)(2,1)}) %all-gather.8.cloned.1.call-update) | async-done | bytes 4194320 | tf_op jit(solution)/shard_map/all_gather | solution.py:47
  392.4 46.7 %all-gather.20.cloned.1.call-done = f32[1024,1024]{1,0:T(8,128)} async-done(((f32[128,1024]{1,0:T(8,128)}), f32[1024,1024]{1,0:T(8,128)}) %all-gather.20.cloned.1.call-update) | async-done | bytes 4194320 | tf_op jit(solution)/shard_map/all_gather | solution.py:41
  439.1 16.8 %fusion.32 = f32[2048,1024]{1,0:T(8,128)S(1)} fusion(bf16[2048,1024]{1,0:T(8,128)(2,1)} %all-gather.8.cloned.1.call-done, f32[1024,1024]{1,0:T(8,128)} %all-gather.20.cloned.1.call-done), kind=kOutput, calls=%fused_computation.43 | convolution fusion | flops 25769803776 | bytes 16777216 | tf_op jit(solution)/shard_map/dot_general | solution.py:48
  455.9 0.0 copy-done.1
  455.9 0.0 copy-done
  455.9 0.0 copy-done.2
  455.9 30.5 %multiply_convert_fusion = bf16[2048,1024]{1,0:T(8,128)(2,1)} fusion(bf16[2048,1024]{1,0:T(8,128)(2,1)S(1)} %copy-done.2, s32[2048,1024]{1,0:T(8,128)} %param.5, f32[2048,1024]{1,0:T(8,128)S(1)} %fusion.32, f32[896,1024]{1,0:T(8,128)S(1)} %copy-done, f32[128,1024]{1,0:T(8,128)S(1)} %copy-done.1), kind=kOutput, calls=%fused_computation.1 | convolution fusion | flops 25781338112 | bytes 29360128 | tf_op jit(solution)/shard_map/dot_general | solution.py:49
  (4 shorter events, 0.0 us)
Async XLA Ops:
  6.5 53.0 %all-gather.10.cloned.1.call-start = ((), (), s32[]{:S(2)}) async-start(), calls=%async_computation.1 | async-start | bytes 4718592 | tf_op jit(solution)/shard_map/all_gather | solution.py:19
  8.4 163.8 %all-reduce.3.cloned.1.call-start = ((), (), s32[]{:S(2)}) async-start(), calls=%async_computation.7 | async-start | bytes 8388608 | tf_op jit(solution)/shard_map/psum | solution.py:23
  70.2 150.9 %all-gather.12.cloned.1.call-start = ((), (), s32[]{:S(2)}) async-start(), calls=%async_computation.2 | async-start | bytes 4718592 | tf_op jit(solution)/shard_map/all_gather | solution.py:24
  174.1 105.3 %all-gather.14.cloned.1.call-start = ((), (), s32[]{:S(2)}) async-start(), calls=%async_computation.3 | async-start | bytes 2359296 | tf_op jit(solution)/shard_map/all_gather | solution.py:36
  251.3 60.2 %all-gather.16.cloned.1.call-start = ((), (), s32[]{:S(2)}) async-start(), calls=%async_computation.4 | async-start | bytes 2359296 | tf_op jit(solution)/shard_map/all_gather | solution.py:36
  282.8 60.8 %all-gather.18.cloned.1.call-start = ((), (), s32[]{:S(2)}) async-start(), calls=%async_computation.5 | async-start | bytes 2359296 | tf_op jit(solution)/shard_map/all_gather | solution.py:36
  314.9 77.5 %all-gather.8.cloned.1.call-start = ((), (), s32[]{:S(2)}) async-start(), calls=%async_computation | async-start | bytes 4718592 | tf_op jit(solution)/shard_map/all_gather | solution.py:47
  317.2 121.8 %all-gather.20.cloned.1.call-start = ((), (), s32[]{:S(2)}) async-start(), calls=%async_computation.6 | async-start | bytes 4718592 | tf_op jit(solution)/shard_map/all_gather | solution.py:41
  351.6 104.3 %copy-start.1 = (f32[128,1024]{1,0:T(8,128)S(1)}, f32[128,1024]{1,0:T(8,128)}, u32[]{:S(2)}) copy-start(f32[128,1024]{1,0:T(8,128)} %broadcast_multiply_fusion.1) | copy-start | bytes 1572868
  439.1 16.8 %copy-start = (f32[896,1024]{1,0:T(8,128)S(1)}, f32[896,1024]{1,0:T(8,128)}, u32[]{:S(2)}) copy-start(f32[896,1024]{1,0:T(8,128)} %broadcast_multiply_fusion) | copy-start | bytes 11010052
  439.1 16.8 %copy-start.2 = (bf16[2048,1024]{1,0:T(8,128)(2,1)S(1)}, bf16[2048,1024]{1,0:T(8,128)(2,1)}, u32[]{:S(2)}) copy-start(bf16[2048,1024]{1,0:T(8,128)(2,1)} %param.4) | copy-start | bytes 12582916
Sparse Core Ops, SparseCore 0:
  8.9 50.5 all-gather.9
  70.3 101.8 all-reduce.2
  174.3 46.8 all-gather.11
  251.4 27.9 all-gather.13
  282.9 28.6 all-gather.15
  315.0 28.5 all-gather.17
  345.2 47.2 all-gather.7
  394.0 45.0 all-gather.19
where the time goes:
time: 494 us; the launch traced here: 493 us
  waiting for transfers between devices  356 us (72%)
  matrix products  86.3 us (17%)
  local copies, waits for them, and re-layouts  22.1 us (4%)
  between operations  14.9 us (3%)
  other arithmetic  13.3 us (3%)
    psum x1, waiting for transfers between devices, per_device(): block_part = lax.psum(partial_panel[:panel_width], 'tok') / total_count  102 us
    all_gather x3, waiting for transfers between devices, per_device(): lax.all_gather(iterate.astype(jnp.bfloat16), 'col', axis=0, tiled=True)  68.8 us
    all_gather x1, waiting for transfers between devices, per_device(): lax.all_gather(activations[:, :panel_width], 'col', axis=1, tiled=True)  51 us
    all_gather x1, waiting for transfers between devices, per_device(): diagonal_block = lax.all_gather(block_part, 'col', axis=0, tiled=True)  46.9 us
    all_gather x1, waiting for transfers between devices, per_device(): inverse = lax.all_gather(iterate, 'col', axis=0, tiled=True)  46.7 us
    all_gather x1, waiting for transfers between devices, per_device(): lax.all_gather(pruned, 'col', axis=1, tiled=True).astype(jnp.float32)  40.8 us
    dot_general x1, matrix products, per_device(): lax.dot_general(factor_rows, hessian_panel, (((1,), (1,)), ((), ())), pre...  30.5 us
    dot_general x4, matrix products, per_device(): product = jnp.dot(iterate, damped, precision=highest)  18.8 us
  transfers between devices with their start and end apart: 8, of which 8 were waited for; matrix products, arithmetic and copies ran while one was open for 5% of the time, Pallas kernels for 0%

commit v1 on v0

--- a/solution.py
+++ b/solution.py
@@ -14,9 +14,12 @@
     tok_rows = activations.shape[0]
     panel_width = B // n_col
     total_count = tok_rows * n_tok
+    _connect_kinds = lambda in_dim, chunk, bus_axis: jnp.concatenate(
+        lax.all_gather(chunk, bus_axis), in_dim
+    )
     partial_panel = lax.dot_general(
         activations,
-        lax.all_gather(activations[:, :panel_width], "col", axis=1, tiled=True),
+        _connect_kinds(1, activations[:, :panel_width], "col"),
         (((0,), (0,)), ((), ())),
         preferred_element_type=jnp.float32,
     )

time: 494 us -> 501 us (1.014)
  local copies, waits for them, and re-layouts: 22.1 us -> 28.5 us
    reshape x0 -> x1, local copies, waits for them, and re-layouts: none -> 6.43 us  [per_device(): jnp.concatenate(lax.all_gather(chunk, bus_axis), in_dim)]
where the time goes in v1:
time: 501 us; the launch traced here: 499 us
  waiting for transfers between devices  356 us (71%)
  matrix products  86.4 us (17%)
  local copies, waits for them, and re-layouts  28.5 us (6%)
  between operations  14.9 us (3%)
  other arithmetic  13.3 us (3%)
    psum x1, waiting for transfers between devices, per_device(): block_part = lax.psum(partial_panel[:panel_width], 'tok') / total_count  103 us
    all_gather x3, waiting for transfers between devices, per_device(): lax.all_gather(iterate.astype(jnp.bfloat16), 'col', axis=0, tiled=True)  68.5 us
    all_gather x1, waiting for transfers between devices, per_device(): lax.all_gather(chunk, bus_axis)  50.1 us
    all_gather x1, waiting for transfers between devices, per_device(): diagonal_block = lax.all_gather(block_part, 'col', axis=0, tiled=True)  46.9 us
    all_gather x1, waiting for transfers between devices, per_device(): inverse = lax.all_gather(iterate, 'col', axis=0, tiled=True)  46.7 us
    all_gather x1, waiting for transfers between devices, per_device(): lax.all_gather(pruned, 'col', axis=1, tiled=True).astype(jnp.float32)  40.8 us
    dot_general x1, matrix products, per_device(): lax.dot_general(factor_rows, hessian_panel, (((1,), (1,)), ((), ())), pre...  30.6 us
    dot_general x4, matrix products, per_device(): product = jnp.dot(iterate, damped, precision=highest)  18.8 us
  transfers between devices with their start and end apart: 8, of which 8 were waited for; matrix products, arithmetic and copies ran while one was open for 5% of the time, Pallas kernels for 0%

profile of v1, /device:TPU:0, one launch (start us, length us, event | category | flops | bytes accessed | tf_op | source)
XLA Modules:
  0.0 499.5 jit_solution(12740243283955924058)
XLA Ops:
  6.5 0.0 all-gather.21.cloned.1.call-start
  6.5 1.9 slice.17
  8.4 0.0 all-gather.21.cloned.1.call-update
  8.4 0.0 all-reduce.3.cloned.1.call-start
  8.5 50.1 %all-gather.21.cloned.1.call-done = bf16[16384,128]{1,0:T(8,128)(2,1)} async-done(((bf16[2048,128]{1,0:T(8,128)(2,1)}), bf16[16384,128]{1,0:T(8,128)(2,1)}) %all-gather.21.cloned.1.call-update) | async-done | bytes 4194320 | tf_op jit(solution)/shard_map/all_gather | solution.py:18
  58.6 6.4 %copy.4 = bf16[2048,8,128]{0,2,1:T(8,128)(2,1)} copy(bf16[2048,8,128]{2,0,1:T(8,128)(2,1)} %bitcast.21) | data formatting | bytes 8388608 | tf_op jit(solution)/shard_map/reshape | solution.py:17
  65.0 7.6 %fusion.31 = f32[1024,1024]{1,0:T(8,128)S(1)} fusion(bf16[2048,1024]{1,0:T(8,128)(2,1)} %param.3, bf16[2048,1024]{0,1:T(8,128)(2,1)} %bitcast.22), kind=kOutput, calls=%fused_computation.42 | convolution fusion | flops 4294967296 | bytes 12582912 | tf_op jit(solution)/shard_map/dot_general | solution.py:20
  72.6 0.8 slice.22
  73.5 2.3 slice.23
  75.7 0.0 all-reduce.3.cloned.1.call-update
  75.8 0.0 all-gather.11.cloned.1.call-start
  75.8 102.5 %all-reduce.3.cloned.1.call-done = (f32[128,1024]{1,0:T(8,128)}, f32[896,1024]{1,0:T(8,128)}) async-done(((f32[128,1024]{1,0:T(8,128)}, f32[896,1024]{1,0:T(8,128)}), (f32[128,1024]{1,0:T(8,128)}, f32[896,1024]{1,0:T(8,128)})) %all-reduce.3.cloned.1.call-update) | async-done | bytes 4194320 | tf_op jit(solution)/shard_map/psum | solution.py:26
  178.4 1.9 broadcast_multiply_fusion.1
  180.3 0.0 all-gather.11.cloned.1.call-update
  180.3 0.0 all-gather.13.cloned.1.call-start
  180.4 46.9 %all-gather.11.cloned.1.call-done = f32[1024,1024]{1,0:T(8,128)} async-done(((f32[128,1024]{1,0:T(8,128)}), f32[1024,1024]{1,0:T(8,128)}) %all-gather.11.cloned.1.call-update) | async-done | bytes 4194320 | tf_op jit(solution)/shard_map/all_gather | solution.py:27
  227.3 17.1 %gather_fusion = f32[1024]{0:T(1024)S(1)} fusion(f32[1024,1024]{1,0:T(8,128)} %all-gather.11.cloned.1.call-done, s32[1024]{0:T(1024)S(1)} %bitcast.20), kind=kCustom, calls=%fused_computation | custom fusion | bytes 16384 | tf_op jit(solution)/shard_map/jit(diagonal)/cond/branch_0_fun/gather | solution.py:29
  244.4 0.6 reduce_sum.18
  245.6 3.9 multiply_reduce_fusion
  250.2 4.7 fusion.16
  254.9 2.5 fusion.28
  257.4 0.0 all-gather.13.cloned.1.call-update
  257.5 0.2 all-gather.15.cloned.1.call-start
  257.7 4.7 fusion.15
  262.4 23.2 %all-gather.13.cloned.1.call-done = bf16[1024,1024]{1,0:T(8,128)(2,1)} async-done(((bf16[128,1024]{1,0:T(8,128)(2,1)}), bf16[1024,1024]{1,0:T(8,128)(2,1)}) %all-gather.13.cloned.1.call-update) | async-done | bytes 2097168 | tf_op jit(solution)/shard_map/all_gather | solution.py:39
  285.6 3.3 fusion.29
  288.9 0.0 all-gather.15.cloned.1.call-update
  288.9 0.0 all-gather.17.cloned.1.call-start
  289.0 4.7 fusion.14
  293.7 24.0 %all-gather.15.cloned.1.call-done = bf16[1024,1024]{1,0:T(8,128)(2,1)} async-done(((bf16[128,1024]{1,0:T(8,128)(2,1)}), bf16[1024,1024]{1,0:T(8,128)(2,1)}) %all-gather.15.cloned.1.call-update) | async-done | bytes 2097168 | tf_op jit(solution)/shard_map/all_gather | solution.py:39
  317.6 3.3 fusion.30
  321.0 0.0 all-gather.17.cloned.1.call-update
  321.0 0.0 all-gather.9.cloned.1.call-start
  321.0 2.3 fusion.17
  323.3 0.0 all-gather.9.cloned.1.call-update
  323.3 0.3 all-gather.19.cloned.1.call-start
  323.6 4.7 fusion.13
  328.3 21.4 %all-gather.17.cloned.1.call-done = bf16[1024,1024]{1,0:T(8,128)(2,1)} async-done(((bf16[128,1024]{1,0:T(8,128)(2,1)}), bf16[1024,1024]{1,0:T(8,128)(2,1)}) %all-gather.17.cloned.1.call-update) | async-done | bytes 2097168 | tf_op jit(solution)/shard_map/all_gather | solution.py:39
  349.7 3.4 convolution_subtract_fusion
  353.1 0.0 all-gather.19.cloned.1.call-update
  353.1 4.6 broadcast_multiply_fusion
  357.7 40.8 %all-gather.9.cloned.1.call-done = bf16[2048,1024]{1,0:T(8,128)(2,1)} async-done(((bf16[2048,128]{1,0:T(8,128)(2,1)}), bf16[2048,1024]{1,0:T(8,128)(2,1)}) %all-gather.9.cloned.1.call-update) | async-done | bytes 4194320 | tf_op jit(solution)/shard_map/all_gather | solution.py:50
  398.5 46.7 %all-gather.19.cloned.1.call-done = f32[1024,1024]{1,0:T(8,128)} async-done(((f32[128,1024]{1,0:T(8,128)}), f32[1024,1024]{1,0:T(8,128)}) %all-gather.19.cloned.1.call-update) | async-done | bytes 4194320 | tf_op jit(solution)/shard_map/all_gather | solution.py:44
  445.2 16.8 %fusion.32 = f32[2048,1024]{1,0:T(8,128)S(1)} fusion(bf16[2048,1024]{1,0:T(8,128)(2,1)} %all-gather.9.cloned.1.call-done, f32[1024,1024]{1,0:T(8,128)} %all-gather.19.cloned.1.call-done), kind=kOutput, calls=%fused_computation.43 | convolution fusion | flops 25769803776 | bytes 16777216 | tf_op jit(solution)/shard_map/dot_general | solution.py:51
  462.0 0.0 copy-done.1
  462.0 0.0 copy-done
  462.0 0.0 copy-done.2
  462.0 30.6 %multiply_convert_fusion = bf16[2048,1024]{1,0:T(8,128)(2,1)} fusion(bf16[2048,1024]{1,0:T(8,128)(2,1)S(1)} %copy-done.2, s32[2048,1024]{1,0:T(8,128)} %param.5, f32[2048,1024]{1,0:T(8,128)S(1)} %fusion.32, f32[896,1024]{1,0:T(8,128)S(1)} %copy-done, f32[128,1024]{1,0:T(8,128)S(1)} %copy-done.1), kind=kOutput, calls=%fused_computation.1 | convolution fusion | flops 25781338112 | bytes 29360128 | tf_op jit(solution)/shard_map/dot_general | solution.py:52
  (5 shorter events, 0.0 us)
Async XLA Ops:
  6.5 52.0 %all-gather.21.cloned.1.call-start = ((), (), s32[]{:S(2)}) async-start(), calls=%async_computation.6 | async-start | bytes 4718592 | tf_op jit(solution)/shard_map/all_gather | solution.py:18
  8.4 169.9 %all-reduce.3.cloned.1.call-start = ((), (), s32[]{:S(2)}) async-start(), calls=%async_computation.7 | async-start | bytes 8388608 | tf_op jit(solution)/shard_map/psum | solution.py:26
  75.8 151.5 %all-gather.11.cloned.1.call-start = ((), (), s32[]{:S(2)}) async-start(), calls=%async_computation.1 | async-start | bytes 4718592 | tf_op jit(solution)/shard_map/all_gather | solution.py:27
  180.3 105.3 %all-gather.13.cloned.1.call-start = ((), (), s32[]{:S(2)}) async-start(), calls=%async_computation.2 | async-start | bytes 2359296 | tf_op jit(solution)/shard_map/all_gather | solution.py:39
  257.5 60.2 %all-gather.15.cloned.1.call-start = ((), (), s32[]{:S(2)}) async-start(), calls=%async_computation.3 | async-start | bytes 2359296 | tf_op jit(solution)/shard_map/all_gather | solution.py:39
  288.9 60.8 %all-gather.17.cloned.1.call-start = ((), (), s32[]{:S(2)}) async-start(), calls=%async_computation.4 | async-start | bytes 2359296 | tf_op jit(solution)/shard_map/all_gather | solution.py:39
  321.0 77.5 %all-gather.9.cloned.1.call-start = ((), (), s32[]{:S(2)}) async-start(), calls=%async_computation | async-start | bytes 4718592 | tf_op jit(solution)/shard_map/all_gather | solution.py:50
  323.3 121.8 %all-gather.19.cloned.1.call-start = ((), (), s32[]{:S(2)}) async-start(), calls=%async_computation.5 | async-start | bytes 4718592 | tf_op jit(solution)/shard_map/all_gather | solution.py:44
  357.7 104.3 %copy-start.1 = (f32[128,1024]{1,0:T(8,128)S(1)}, f32[128,1024]{1,0:T(8,128)}, u32[]{:S(2)}) copy-start(f32[128,1024]{1,0:T(8,128)} %broadcast_multiply_fusion.1) | copy-start | bytes 1572868
  445.2 16.8 %copy-start = (f32[896,1024]{1,0:T(8,128)S(1)}, f32[896,1024]{1,0:T(8,128)}, u32[]{:S(2)}) copy-start(f32[896,1024]{1,0:T(8,128)} %broadcast_multiply_fusion) | copy-start | bytes 11010052
  445.2 16.8 %copy-start.2 = (bf16[2048,1024]{1,0:T(8,128)(2,1)S(1)}, bf16[2048,1024]{1,0:T(8,128)(2,1)}, u32[]{:S(2)}) copy-start(bf16[2048,1024]{1,0:T(8,128)(2,1)} %param.4) | copy-start | bytes 12582916
Sparse Core Ops, SparseCore 0:
  8.9 49.5 all-gather.20
  75.9 102.4 all-reduce.2
  180.4 46.8 all-gather.10
  257.6 27.9 all-gather.12
  289.1 28.5 all-gather.14
  321.1 28.5 all-gather.16
  351.3 47.1 all-gather.8
  400.1 45.0 all-gather.18
